TPU v7x, 32 devices: a whole 2x2x4 slice. The times are simulated.
32 devices in a mesh: section: 2 (over core), dp: 4 (over y, x), tensor: 4 (over z).
Axes of the slice: x: 2, y: 2, z: 4, core: 2. Of those that a mesh axis runs over, the one named last changes fastest.
Arguments:
- section_input: bfloat16 [2, 512, 4096], P('section', 'dp'), may hold values from -60 to 60
- weights: bfloat16 [2, 4096, 4096], P('section', 'tensor', 'dp'), may hold values from -0.1875 to 0.1875
- gains: float32 [2, 4096], P('section'), may hold values from 0.1 to 1.9
- proj_seeds: int32 [2, 2], P('section'), may hold values from 0 to 99999
- out_grad: bfloat16 [512, 4096], P('dp'), may hold values from -0.75 to 0.75
- query_grads: bfloat16 [2, 256, 4096], P('section', 'dp', 'tensor'), may hold values from -0.017944336 to 0.017944336
Outputs:
- projected_grads: float32 [2, 2, 4096], P('section', None, 'tensor')
- scores: float32 [2, 256], P(None, 'dp')
All inputs are finite; a program needn't handle non-finite values.
Results may differ from a plain program's by a relative error of at most 0.033.
Values may be sent and summed in bfloat16 or wider, within the bound.
A program may use at most 64 MiB of HBM per device.

v0:
```python
import math
import jax
import jax.numpy as jnp
from jax import lax
from jax.sharding import PartitionSpec as P

R = 64
SEQS = 2
MICRO = 16
eps = 1e-05


def passed_along(value, axis, steps):
    count = lax.axis_size(axis)
    first, last = (max(0, -steps), min(count, count - steps))
    return lax.ppermute(value, axis, [(source, source + steps) for source in range(first, last)])


def sign_table(seed_value, row_count):
    row_index = lax.broadcasted_iota(jnp.int32, (row_count, R), 0)
    col_index = lax.broadcasted_iota(jnp.int32, (row_count, R), 1)
    mixing = row_index * 40503 + col_index * 9973 + seed_value * 7919 + 12345
    mixing = mixing ^ mixing >> 13
    mixing = mixing * 1274126177
    mixing = mixing ^ mixing >> 16
    parity = mixing >> 10 & 1
    return (jnp.where(parity == 1, 1.0, -1.0) * (1.0 / math.sqrt(row_count))).astype(jnp.bfloat16)


def take_rows(table, row_start):
    return lax.dynamic_slice_in_dim(table, row_start, MICRO, 0)


def body(section_input, weights, gains, proj_seeds, out_grad, query_grads):
    section_count = lax.axis_size("section")
    section_index = lax.axis_index("section")
    data_count = lax.axis_size("dp")
    data_index = lax.axis_index("dp")
    split_count = lax.axis_size("tensor")
    split_index = lax.axis_index("tensor")
    tok_rows = section_input.shape[1]
    feature_width = section_input.shape[2]
    slice_width = feature_width // split_count
    blocks = tok_rows // MICRO
    turn_count = section_count + blocks - 1
    own_start = split_index * slice_width
    gain_row = gains[0]
    hidden_in = section_input[0].astype(jnp.float32)
    radius = jnp.sqrt(jnp.mean(hidden_in * hidden_in, axis=1, keepdims=True) + eps)
    normed = hidden_in / radius
    lifted = (normed * gain_row).astype(jnp.bfloat16)
    weight_rows = lax.all_gather(weights[0], "dp", axis=1, tiled=True)
    lifted_own = lax.dynamic_slice_in_dim(lifted, own_start, slice_width, 1)
    partial_value = jnp.dot(lifted_own, weight_rows, preferred_element_type=jnp.float32)
    summed = lax.psum(partial_value.astype(jnp.bfloat16), "tensor").astype(jnp.float32)
    sigmoid_z = jax.nn.sigmoid(summed)
    slopes = sigmoid_z * (1.0 + summed * (1.0 - sigmoid_z))
    proj_in = sign_table(proj_seeds[0, 0], feature_width)
    proj_out = sign_table(proj_seeds[0, 1], feature_width)
    in_features = jnp.dot(lifted, proj_in, preferred_element_type=jnp.float32).astype(jnp.bfloat16)
    chain_depth = section_count - 1 - section_index
    at_top = section_index == section_count - 1

    def block_grad(operands):
        upstream, slope_rows, feature_rows, grad_sum = operands
        grad_pre = (upstream.astype(jnp.float32) * slope_rows).astype(jnp.bfloat16)
        out_features = jnp.dot(grad_pre, proj_out, preferred_element_type=jnp.float32).astype(
            jnp.bfloat16
        )
        grad_sum = grad_sum + lax.dot_general(
            feature_rows, out_features, (((0,), (0,)), ((), ())), preferred_element_type=jnp.float32
        )
        own_grads = lax.dot_general(
            grad_pre, weight_rows, (((1,), (1,)), ((), ())), preferred_element_type=jnp.float32
        ).astype(jnp.bfloat16)
        return (own_grads, grad_sum)

    def block_skip(operands):
        return (jnp.zeros((MICRO, slice_width), jnp.bfloat16), operands[3])

    def prepare(turn_index, upstream_in):
        block_index = turn_index.astype(jnp.int32) - chain_depth
        active = jnp.logical_and(block_index >= 0, block_index < blocks)
        row_start = jnp.clip(block_index, 0, blocks - 1) * MICRO
        top_rows = take_rows(out_grad, row_start)
        upstream = jnp.where(at_top, top_rows, upstream_in)
        return (active, row_start, upstream)

    def turn(turn_index, loop_state):
        incoming, grad_sum = loop_state
        active, row_start, upstream = prepare(turn_index, incoming)
        own_grads, grad_sum = lax.cond(
            active,
            block_grad,
            block_skip,
            (upstream, take_rows(slopes, row_start), take_rows(in_features, row_start), grad_sum),
        )
        full_grads = lax.all_gather(own_grads, "tensor", axis=1, tiled=True)

        def finish(operands):
            upstream_rows, grad_rows, normed_rows, radius_rows = operands
            scaled = grad_rows.astype(jnp.float32) * gain_row
            mean_dot = jnp.mean(scaled * normed_rows, axis=1, keepdims=True)
            return (
                upstream_rows.astype(jnp.float32) + (scaled - normed_rows * mean_dot) / radius_rows
            ).astype(jnp.bfloat16)

        def vacant(operands):
            return jnp.zeros((MICRO, feature_width), jnp.bfloat16)

        outgoing = lax.cond(
            active,
            finish,
            vacant,
            (upstream, full_grads, take_rows(normed, row_start), take_rows(radius, row_start)),
        )
        received = passed_along(outgoing, "section", -1)
        return (received, grad_sum)

    start_state = (jnp.zeros((MICRO, feature_width), jnp.bfloat16), jnp.zeros((R, R), jnp.float32))
    received, grad_sum = lax.fori_loop(0, turn_count, turn, start_state)
    flattened = grad_sum.reshape(R * R)
    piece_width = R * R // split_count
    own_part = lax.dynamic_slice_in_dim(flattened, split_index * piece_width, piece_width, 0)
    seq_index = data_index // (data_count // SEQS)
    seq_mask = (lax.broadcasted_iota(jnp.int32, (SEQS, 1), 0) == seq_index).astype(jnp.float32)
    per_seq = seq_mask * own_part[None, :]
    grads_all = lax.psum(per_seq, "dp")
    queries = query_grads[0].astype(jnp.float32)
    partial_scores = jnp.dot(grads_all, queries.T, precision=lax.Precision.HIGHEST)
    scores = lax.psum(partial_scores, ("section", "tensor"))
    return (grads_all[None], scores)


def solution(mesh):
    in_specs = (
        P("section", "dp", None),
        P("section", "tensor", "dp"),
        P("section", None),
        P("section", None),
        P("dp", None),
        P("section", "dp", "tensor"),
    )
    out_specs = (P("section", None, "tensor"), P(None, "dp"))
    return jax.shard_map(body, mesh=mesh, in_specs=in_specs, out_specs=out_specs, check_vma=False)
```

profile of v0, /device:TPU:1, one launch (start us, length us, event | category | flops | bytes accessed | tf_op | source)
XLA Modules:
  0.0 457.9 jit_solution(3057841927889815034)
XLA Ops:
  11.0 88.2 %all-gather.3.cloned.1.call-done = bf16[1,1024,4096]{2,1,0:T(8,128)(2,1)} async-done(((bf16[1,1024,1024]{2,1,0:T(8,128)(2,1)}), bf16[1,1024,4096]{2,1,0:T(8,128)(2,1)}) %all-gather.3.cloned.1.call-update) | async-done | bytes 8388624 | tf_op jit(solution)/shard_map/all_gather | solution.py:52
  99.3 5.7 %convolution_convert_fusion.2 = bf16[128,4096]{1,0:T(8,128)(2,1)} fusion(bf16[128,4096]{1,0:T(8,128)(2,1)S(1)} %get-tuple-element.421, s32[]{:T(128)S(6)} %select_n.44, bf16[1,1024,4096]{2,1,0:T(8,128)(2,1)} %all-gather.3.cloned.1.call-done), kind=kOutput, calls=%fused_computation.21 | convolution fusion | flops 1074266112 | bytes 9699332 | tf_op jit(solution)/shard_map/dot_general | solution.py:54
  108.1 2.1 convolution_convert_fusion.3
  111.4 45.8 %all-reduce.2.cloned.1.call-done = bf16[128,4096]{1,0:T(8,128)(2,1)} async-done(((bf16[128,4096]{1,0:T(8,128)(2,1)}), bf16[128,4096]{1,0:T(8,128)(2,1)}) %all-reduce.2.cloned.1.call-update) | async-done | bytes 1048592 | tf_op jit(solution)/shard_map/psum | solution.py:55
  157.3 1.9 fusion.13
  159.8 263.6 %while.19 = (s32[]{:T(128)}, bf16[16,4096]{1,0:T(8,128)(2,1)S(1)}, f32[64,64]{1,0:T(8,128)}, s32[]{:T(128)}, pred[]{:T(512)}, /*index=5*/bf16[128,4096]{1,0:T(8,...) while((s32[]{:T(128)}, bf16[16,4096]{1,0:T(8,128)(2,1)S(1)}, ...), condition=%wide.region_8.9_spmd.clone, body=%wide.region_2.8_spmd.clone.sunk | while | flops 147674128 | bytes 13017286 | solution.py:121
  159.9 2.3 multiply_convert_fusion.9
  163.2 7.4 %conditional.6 = (bf16[16,1024]{1,0:T(8,128)(2,1)S(1)}, f32[64,64]{1,0:T(8,128)}) conditional(s32[]{:T(128)} %convert_element_type.134, f32[64,64]{1,0:T(8,128)} %get-tuple-element.548, (bf16[16,4096]{1,0:T(8,128)(2,1)S(1)}, f32[128,4096]{1,0:T(8,128)S(1)}, s32[]{:T(128)}, bf16[1024,4096]{1,0:T(8,128)(2,1)}, bf16[128,64]{1,0:T(8,128)(2,1)}, ...), branch_computations={%region_3.3_spmd, %region_4.4_spmd} | conditional | flops 143152128 | bytes 10310676 | solution.py:92
  163.2 5.6 %convolution_convert_fusion = bf16[16,1024]{1,0:T(8,128)(2,1)S(1)} fusion(bf16[1024,4096]{1,0:T(8,128)(2,1)} %get-tuple-element.308, f32[128,4096]{1,0:T(8,128)S(1)} %get-tuple-element.306, s32[]{:T(128)} %get-tuple-element.307, bf16[16,4096]{1,0:T(8,128)(2,1)S(1)} %get-tuple-element.305), kind=kOutput, calls=%fused_computation.1 | convolution fusion | flops 134430720 | bytes 8814596 | tf_op jit(solution)/shard_map/while/body/eval_jaxpr/cond/branch_1_fun/dot_general | solution.py:73
  168.8 1.8 convolution_add_fusion
  170.6 10.4 %all_gather.13 = bf16[16,4096]{1,0:T(8,128)(2,1)S(1)} all-gather(bf16[16,1024]{1,0:T(8,128)(2,1)S(1)} %get-tuple-element.519), channel_id=1, replica_groups=mesh['section'=2,'dp'=4,'tensor'=4] {'tensor'}, dimensions={1}, use_global_device_ids=true | all-gather | bytes 163840 | tf_op jit(solution)/shard_map/while/body/eval_jaxpr/all_gather | solution.py:98
  181.1 2.4 conditional.7
  185.7 2.3 multiply_convert_fusion.9
  189.0 7.4 %conditional.6 = (bf16[16,1024]{1,0:T(8,128)(2,1)S(1)}, f32[64,64]{1,0:T(8,128)}) conditional(s32[]{:T(128)} %convert_element_type.134, f32[64,64]{1,0:T(8,128)} %get-tuple-element.548, (bf16[16,4096]{1,0:T(8,128)(2,1)S(1)}, f32[128,4096]{1,0:T(8,128)S(1)}, s32[]{:T(128)}, bf16[1024,4096]{1,0:T(8,128)(2,1)}, bf16[128,64]{1,0:T(8,128)(2,1)}, ...), branch_computations={%region_3.3_spmd, %region_4.4_spmd} | conditional | flops 143152128 | bytes 10310676 | solution.py:92
  189.0 5.6 %convolution_convert_fusion = bf16[16,1024]{1,0:T(8,128)(2,1)S(1)} fusion(bf16[1024,4096]{1,0:T(8,128)(2,1)} %get-tuple-element.308, f32[128,4096]{1,0:T(8,128)S(1)} %get-tuple-element.306, s32[]{:T(128)} %get-tuple-element.307, bf16[16,4096]{1,0:T(8,128)(2,1)S(1)} %get-tuple-element.305), kind=kOutput, calls=%fused_computation.1 | convolution fusion | flops 134430720 | bytes 8814596 | tf_op jit(solution)/shard_map/while/body/eval_jaxpr/cond/branch_1_fun/dot_general | solution.py:73
  194.7 1.8 convolution_add_fusion
  196.4 10.5 %all_gather.13 = bf16[16,4096]{1,0:T(8,128)(2,1)S(1)} all-gather(bf16[16,1024]{1,0:T(8,128)(2,1)S(1)} %get-tuple-element.519), channel_id=1, replica_groups=mesh['section'=2,'dp'=4,'tensor'=4] {'tensor'}, dimensions={1}, use_global_device_ids=true | all-gather | bytes 163840 | tf_op jit(solution)/shard_map/while/body/eval_jaxpr/all_gather | solution.py:98
  206.9 2.4 conditional.7
  209.3 5.2 %collective-permute-start = (bf16[16,4096]{1,0:T(8,128)(2,1)S(1)}, bf16[16,4096]{1,0:T(8,128)(2,1)S(1)}, u32[]{:S(2)}, u32[]{:S(2)}) collective-permute-start(bf16[16,4096]{1,0:T(8,128)(2,1)S(1)} %get-tuple-element.588), channel_id=1, source_target_pairs={{16,0},{17,1},{18,2},{19,3},{20,4},{21,5},{22,6},{23,7},{24,8},{25... | collective-permute-start | bytes 393224 | tf_op jit(solution)/shard_map/while/body/eval_jaxpr/ppermute | solution.py:16
  215.5 2.3 multiply_convert_fusion.9
  218.8 7.4 %conditional.6 = (bf16[16,1024]{1,0:T(8,128)(2,1)S(1)}, f32[64,64]{1,0:T(8,128)}) conditional(s32[]{:T(128)} %convert_element_type.134, f32[64,64]{1,0:T(8,128)} %get-tuple-element.548, (bf16[16,4096]{1,0:T(8,128)(2,1)S(1)}, f32[128,4096]{1,0:T(8,128)S(1)}, s32[]{:T(128)}, bf16[1024,4096]{1,0:T(8,128)(2,1)}, bf16[128,64]{1,0:T(8,128)(2,1)}, ...), branch_computations={%region_3.3_spmd, %region_4.4_spmd} | conditional | flops 143152128 | bytes 10310676 | solution.py:92
  218.8 5.6 %convolution_convert_fusion = bf16[16,1024]{1,0:T(8,128)(2,1)S(1)} fusion(bf16[1024,4096]{1,0:T(8,128)(2,1)} %get-tuple-element.308, f32[128,4096]{1,0:T(8,128)S(1)} %get-tuple-element.306, s32[]{:T(128)} %get-tuple-element.307, bf16[16,4096]{1,0:T(8,128)(2,1)S(1)} %get-tuple-element.305), kind=kOutput, calls=%fused_computation.1 | convolution fusion | flops 134430720 | bytes 8814596 | tf_op jit(solution)/shard_map/while/body/eval_jaxpr/cond/branch_1_fun/dot_general | solution.py:73
  224.4 1.8 convolution_add_fusion
  226.2 10.5 %all_gather.13 = bf16[16,4096]{1,0:T(8,128)(2,1)S(1)} all-gather(bf16[16,1024]{1,0:T(8,128)(2,1)S(1)} %get-tuple-element.519), channel_id=1, replica_groups=mesh['section'=2,'dp'=4,'tensor'=4] {'tensor'}, dimensions={1}, use_global_device_ids=true | all-gather | bytes 163840 | tf_op jit(solution)/shard_map/while/body/eval_jaxpr/all_gather | solution.py:98
  236.7 2.4 conditional.7
  239.1 5.2 %collective-permute-start = (bf16[16,4096]{1,0:T(8,128)(2,1)S(1)}, bf16[16,4096]{1,0:T(8,128)(2,1)S(1)}, u32[]{:S(2)}, u32[]{:S(2)}) collective-permute-start(bf16[16,4096]{1,0:T(8,128)(2,1)S(1)} %get-tuple-element.588), channel_id=1, source_target_pairs={{16,0},{17,1},{18,2},{19,3},{20,4},{21,5},{22,6},{23,7},{24,8},{25... | collective-permute-start | bytes 393224 | tf_op jit(solution)/shard_map/while/body/eval_jaxpr/ppermute | solution.py:16
  245.2 2.3 multiply_convert_fusion.9
  248.5 7.4 %conditional.6 = (bf16[16,1024]{1,0:T(8,128)(2,1)S(1)}, f32[64,64]{1,0:T(8,128)}) conditional(s32[]{:T(128)} %convert_element_type.134, f32[64,64]{1,0:T(8,128)} %get-tuple-element.548, (bf16[16,4096]{1,0:T(8,128)(2,1)S(1)}, f32[128,4096]{1,0:T(8,128)S(1)}, s32[]{:T(128)}, bf16[1024,4096]{1,0:T(8,128)(2,1)}, bf16[128,64]{1,0:T(8,128)(2,1)}, ...), branch_computations={%region_3.3_spmd, %region_4.4_spmd} | conditional | flops 143152128 | bytes 10310676 | solution.py:92
  248.5 5.6 %convolution_convert_fusion = bf16[16,1024]{1,0:T(8,128)(2,1)S(1)} fusion(bf16[1024,4096]{1,0:T(8,128)(2,1)} %get-tuple-element.308, f32[128,4096]{1,0:T(8,128)S(1)} %get-tuple-element.306, s32[]{:T(128)} %get-tuple-element.307, bf16[16,4096]{1,0:T(8,128)(2,1)S(1)} %get-tuple-element.305), kind=kOutput, calls=%fused_computation.1 | convolution fusion | flops 134430720 | bytes 8814596 | tf_op jit(solution)/shard_map/while/body/eval_jaxpr/cond/branch_1_fun/dot_general | solution.py:73
  254.2 1.8 convolution_add_fusion
  256.0 10.5 %all_gather.13 = bf16[16,4096]{1,0:T(8,128)(2,1)S(1)} all-gather(bf16[16,1024]{1,0:T(8,128)(2,1)S(1)} %get-tuple-element.519), channel_id=1, replica_groups=mesh['section'=2,'dp'=4,'tensor'=4] {'tensor'}, dimensions={1}, use_global_device_ids=true | all-gather | bytes 163840 | tf_op jit(solution)/shard_map/while/body/eval_jaxpr/all_gather | solution.py:98
  266.4 2.4 conditional.7
  268.8 5.2 %collective-permute-start = (bf16[16,4096]{1,0:T(8,128)(2,1)S(1)}, bf16[16,4096]{1,0:T(8,128)(2,1)S(1)}, u32[]{:S(2)}, u32[]{:S(2)}) collective-permute-start(bf16[16,4096]{1,0:T(8,128)(2,1)S(1)} %get-tuple-element.588), channel_id=1, source_target_pairs={{16,0},{17,1},{18,2},{19,3},{20,4},{21,5},{22,6},{23,7},{24,8},{25... | collective-permute-start | bytes 393224 | tf_op jit(solution)/shard_map/while/body/eval_jaxpr/ppermute | solution.py:16
  275.0 2.3 multiply_convert_fusion.9
  278.2 7.4 %conditional.6 = (bf16[16,1024]{1,0:T(8,128)(2,1)S(1)}, f32[64,64]{1,0:T(8,128)}) conditional(s32[]{:T(128)} %convert_element_type.134, f32[64,64]{1,0:T(8,128)} %get-tuple-element.548, (bf16[16,4096]{1,0:T(8,128)(2,1)S(1)}, f32[128,4096]{1,0:T(8,128)S(1)}, s32[]{:T(128)}, bf16[1024,4096]{1,0:T(8,128)(2,1)}, bf16[128,64]{1,0:T(8,128)(2,1)}, ...), branch_computations={%region_3.3_spmd, %region_4.4_spmd} | conditional | flops 143152128 | bytes 10310676 | solution.py:92
  278.3 5.6 %convolution_convert_fusion = bf16[16,1024]{1,0:T(8,128)(2,1)S(1)} fusion(bf16[1024,4096]{1,0:T(8,128)(2,1)} %get-tuple-element.308, f32[128,4096]{1,0:T(8,128)S(1)} %get-tuple-element.306, s32[]{:T(128)} %get-tuple-element.307, bf16[16,4096]{1,0:T(8,128)(2,1)S(1)} %get-tuple-element.305), kind=kOutput, calls=%fused_computation.1 | convolution fusion | flops 134430720 | bytes 8814596 | tf_op jit(solution)/shard_map/while/body/eval_jaxpr/cond/branch_1_fun/dot_general | solution.py:73
  283.9 1.8 convolution_add_fusion
  285.7 10.5 %all_gather.13 = bf16[16,4096]{1,0:T(8,128)(2,1)S(1)} all-gather(bf16[16,1024]{1,0:T(8,128)(2,1)S(1)} %get-tuple-element.519), channel_id=1, replica_groups=mesh['section'=2,'dp'=4,'tensor'=4] {'tensor'}, dimensions={1}, use_global_device_ids=true | all-gather | bytes 163840 | tf_op jit(solution)/shard_map/while/body/eval_jaxpr/all_gather | solution.py:98
  296.2 2.4 conditional.7
  298.5 5.2 %collective-permute-start = (bf16[16,4096]{1,0:T(8,128)(2,1)S(1)}, bf16[16,4096]{1,0:T(8,128)(2,1)S(1)}, u32[]{:S(2)}, u32[]{:S(2)}) collective-permute-start(bf16[16,4096]{1,0:T(8,128)(2,1)S(1)} %get-tuple-element.588), channel_id=1, source_target_pairs={{16,0},{17,1},{18,2},{19,3},{20,4},{21,5},{22,6},{23,7},{24,8},{25... | collective-permute-start | bytes 393224 | tf_op jit(solution)/shard_map/while/body/eval_jaxpr/ppermute | solution.py:16
  304.7 2.3 multiply_convert_fusion.9
  308.0 7.4 %conditional.6 = (bf16[16,1024]{1,0:T(8,128)(2,1)S(1)}, f32[64,64]{1,0:T(8,128)}) conditional(s32[]{:T(128)} %convert_element_type.134, f32[64,64]{1,0:T(8,128)} %get-tuple-element.548, (bf16[16,4096]{1,0:T(8,128)(2,1)S(1)}, f32[128,4096]{1,0:T(8,128)S(1)}, s32[]{:T(128)}, bf16[1024,4096]{1,0:T(8,128)(2,1)}, bf16[128,64]{1,0:T(8,128)(2,1)}, ...), branch_computations={%region_3.3_spmd, %region_4.4_spmd} | conditional | flops 143152128 | bytes 10310676 | solution.py:92
  308.0 5.6 %convolution_convert_fusion = bf16[16,1024]{1,0:T(8,128)(2,1)S(1)} fusion(bf16[1024,4096]{1,0:T(8,128)(2,1)} %get-tuple-element.308, f32[128,4096]{1,0:T(8,128)S(1)} %get-tuple-element.306, s32[]{:T(128)} %get-tuple-element.307, bf16[16,4096]{1,0:T(8,128)(2,1)S(1)} %get-tuple-element.305), kind=kOutput, calls=%fused_computation.1 | convolution fusion | flops 134430720 | bytes 8814596 | tf_op jit(solution)/shard_map/while/body/eval_jaxpr/cond/branch_1_fun/dot_general | solution.py:73
  313.6 1.8 convolution_add_fusion
  315.4 10.5 %all_gather.13 = bf16[16,4096]{1,0:T(8,128)(2,1)S(1)} all-gather(bf16[16,1024]{1,0:T(8,128)(2,1)S(1)} %get-tuple-element.519), channel_id=1, replica_groups=mesh['section'=2,'dp'=4,'tensor'=4] {'tensor'}, dimensions={1}, use_global_device_ids=true | all-gather | bytes 163840 | tf_op jit(solution)/shard_map/while/body/eval_jaxpr/all_gather | solution.py:98
  325.9 2.4 conditional.7
  328.3 5.2 %collective-permute-start = (bf16[16,4096]{1,0:T(8,128)(2,1)S(1)}, bf16[16,4096]{1,0:T(8,128)(2,1)S(1)}, u32[]{:S(2)}, u32[]{:S(2)}) collective-permute-start(bf16[16,4096]{1,0:T(8,128)(2,1)S(1)} %get-tuple-element.588), channel_id=1, source_target_pairs={{16,0},{17,1},{18,2},{19,3},{20,4},{21,5},{22,6},{23,7},{24,8},{25... | collective-permute-start | bytes 393224 | tf_op jit(solution)/shard_map/while/body/eval_jaxpr/ppermute | solution.py:16
  334.4 2.3 multiply_convert_fusion.9
  337.7 7.4 %conditional.6 = (bf16[16,1024]{1,0:T(8,128)(2,1)S(1)}, f32[64,64]{1,0:T(8,128)}) conditional(s32[]{:T(128)} %convert_element_type.134, f32[64,64]{1,0:T(8,128)} %get-tuple-element.548, (bf16[16,4096]{1,0:T(8,128)(2,1)S(1)}, f32[128,4096]{1,0:T(8,128)S(1)}, s32[]{:T(128)}, bf16[1024,4096]{1,0:T(8,128)(2,1)}, bf16[128,64]{1,0:T(8,128)(2,1)}, ...), branch_computations={%region_3.3_spmd, %region_4.4_spmd} | conditional | flops 143152128 | bytes 10310676 | solution.py:92
  337.7 5.6 %convolution_convert_fusion = bf16[16,1024]{1,0:T(8,128)(2,1)S(1)} fusion(bf16[1024,4096]{1,0:T(8,128)(2,1)} %get-tuple-element.308, f32[128,4096]{1,0:T(8,128)S(1)} %get-tuple-element.306, s32[]{:T(128)} %get-tuple-element.307, bf16[16,4096]{1,0:T(8,128)(2,1)S(1)} %get-tuple-element.305), kind=kOutput, calls=%fused_computation.1 | convolution fusion | flops 134430720 | bytes 8814596 | tf_op jit(solution)/shard_map/while/body/eval_jaxpr/cond/branch_1_fun/dot_general | solution.py:73
  345.1 10.5 %all_gather.13 = bf16[16,4096]{1,0:T(8,128)(2,1)S(1)} all-gather(bf16[16,1024]{1,0:T(8,128)(2,1)S(1)} %get-tuple-element.519), channel_id=1, replica_groups=mesh['section'=2,'dp'=4,'tensor'=4] {'tensor'}, dimensions={1}, use_global_device_ids=true | all-gather | bytes 163840 | tf_op jit(solution)/shard_map/while/body/eval_jaxpr/all_gather | solution.py:98
  355.6 2.4 conditional.7
  358.0 5.2 %collective-permute-start = (bf16[16,4096]{1,0:T(8,128)(2,1)S(1)}, bf16[16,4096]{1,0:T(8,128)(2,1)S(1)}, u32[]{:S(2)}, u32[]{:S(2)}) collective-permute-start(bf16[16,4096]{1,0:T(8,128)(2,1)S(1)} %get-tuple-element.588), channel_id=1, source_target_pairs={{16,0},{17,1},{18,2},{19,3},{20,4},{21,5},{22,6},{23,7},{24,8},{25... | collective-permute-start | bytes 393224 | tf_op jit(solution)/shard_map/while/body/eval_jaxpr/ppermute | solution.py:16
  364.1 2.3 multiply_convert_fusion.9
  367.4 7.4 %conditional.6 = (bf16[16,1024]{1,0:T(8,128)(2,1)S(1)}, f32[64,64]{1,0:T(8,128)}) conditional(s32[]{:T(128)} %convert_element_type.134, f32[64,64]{1,0:T(8,128)} %get-tuple-element.548, (bf16[16,4096]{1,0:T(8,128)(2,1)S(1)}, f32[128,4096]{1,0:T(8,128)S(1)}, s32[]{:T(128)}, bf16[1024,4096]{1,0:T(8,128)(2,1)}, bf16[128,64]{1,0:T(8,128)(2,1)}, ...), branch_computations={%region_3.3_spmd, %region_4.4_spmd} | conditional | flops 143152128 | bytes 10310676 | solution.py:92
  367.4 5.6 %convolution_convert_fusion = bf16[16,1024]{1,0:T(8,128)(2,1)S(1)} fusion(bf16[1024,4096]{1,0:T(8,128)(2,1)} %get-tuple-element.308, f32[128,4096]{1,0:T(8,128)S(1)} %get-tuple-element.306, s32[]{:T(128)} %get-tuple-element.307, bf16[16,4096]{1,0:T(8,128)(2,1)S(1)} %get-tuple-element.305), kind=kOutput, calls=%fused_computation.1 | convolution fusion | flops 134430720 | bytes 8814596 | tf_op jit(solution)/shard_map/while/body/eval_jaxpr/cond/branch_1_fun/dot_general | solution.py:73
  374.9 10.5 %all_gather.13 = bf16[16,4096]{1,0:T(8,128)(2,1)S(1)} all-gather(bf16[16,1024]{1,0:T(8,128)(2,1)S(1)} %get-tuple-element.519), channel_id=1, replica_groups=mesh['section'=2,'dp'=4,'tensor'=4] {'tensor'}, dimensions={1}, use_global_device_ids=true | all-gather | bytes 163840 | tf_op jit(solution)/shard_map/while/body/eval_jaxpr/all_gather | solution.py:98
  385.3 2.3 conditional.7
  387.6 5.3 %collective-permute-start = (bf16[16,4096]{1,0:T(8,128)(2,1)S(1)}, bf16[16,4096]{1,0:T(8,128)(2,1)S(1)}, u32[]{:S(2)}, u32[]{:S(2)}) collective-permute-start(bf16[16,4096]{1,0:T(8,128)(2,1)S(1)} %get-tuple-element.588), channel_id=1, source_target_pairs={{16,0},{17,1},{18,2},{19,3},{20,4},{21,5},{22,6},{23,7},{24,8},{25... | collective-permute-start | bytes 393224 | tf_op jit(solution)/shard_map/while/body/eval_jaxpr/ppermute | solution.py:16
  393.9 2.3 multiply_convert_fusion.9
  397.2 10.5 %all_gather.13 = bf16[16,4096]{1,0:T(8,128)(2,1)S(1)} all-gather(bf16[16,1024]{1,0:T(8,128)(2,1)S(1)} %get-tuple-element.519), channel_id=1, replica_groups=mesh['section'=2,'dp'=4,'tensor'=4] {'tensor'}, dimensions={1}, use_global_device_ids=true | all-gather | bytes 163840 | tf_op jit(solution)/shard_map/while/body/eval_jaxpr/all_gather | solution.py:98
  407.7 14.8 %collective-permute-start = (bf16[16,4096]{1,0:T(8,128)(2,1)S(1)}, bf16[16,4096]{1,0:T(8,128)(2,1)S(1)}, u32[]{:S(2)}, u32[]{:S(2)}) collective-permute-start(bf16[16,4096]{1,0:T(8,128)(2,1)S(1)} %get-tuple-element.588), channel_id=1, source_target_pairs={{16,0},{17,1},{18,2},{19,3},{20,4},{21,5},{22,6},{23,7},{24,8},{25... | collective-permute-start | bytes 393224 | tf_op jit(solution)/shard_map/while/body/eval_jaxpr/ppermute | solution.py:16
  425.0 7.8 %psum.22 = f32[2,1024]{1,0:T(2,128)S(1)} all-reduce(f32[2,1024]{1,0:T(2,128)S(1)} %broadcast_multiply_fusion.1), channel_id=1, replica_groups=mesh['section'=2,'dp'=4,'tensor'=4] {'dp'}, use_global_device_ids=true, to_apply=%region_9.10 | all-reduce | flops 2048 | bytes 16384 | tf_op jit(solution)/shard_map/psum | solution.py:128
  433.0 18.1 %psum.23 = f32[2,64]{1,0:T(2,128)} all-reduce(f32[2,64]{1,0:T(2,128)S(1)} %fusion.32), channel_id=1, replica_groups=mesh['section'=2,'dp'=4,'tensor'=4] {'section','tensor'}, use_global_device_ids=true, to_apply=%region_10.11 | all-reduce | flops 128 | bytes 1024 | tf_op jit(solution)/shard_map/psum | solution.py:131
  (103 shorter events, 50.0 us)
Async XLA Ops:
  7.2 425.6 %copy-start = (bf16[1,64,1024]{2,1,0:T(8,128)(2,1)S(1)}, bf16[1,64,1024]{2,1,0:T(8,128)(2,1)}, u32[]{:S(2)}) copy-start(bf16[1,64,1024]{2,1,0:T(8,128)(2,1)} %param.17) | copy-start | bytes 393220
  7.2 1.3 copy-start.1
  7.2 2.1 copy-start.2
  7.2 92.1 %all-gather.3.cloned.1.call-start = ((), (), s32[]{:S(2)}) async-start(), calls=%async_computation.1 | async-start | bytes 10485760 | tf_op jit(solution)/shard_map/all_gather | solution.py:52
  7.9 149.3 %all-reduce.2.cloned.1.call-start = ((), (), s32[]{:S(2)}) async-start(), calls=%async_computation | async-start | bytes 2097152 | tf_op jit(solution)/shard_map/psum | solution.py:55
  99.3 5.7 %copy-start.4 = (s32[1,2]{1,0:T(1,128)S(1)}, s32[1,2]{1,0:T(1,128)}, u32[]{:S(2)}) copy-start(s32[1,2]{1,0:T(1,128)} %param.15) | copy-start | bytes 28
  163.2 17.9 %copy-start.5 = (f32[128,1]{0,1:T(1,128)S(1)}, f32[128,1]{0,1:T(1,128)}, u32[]{:S(2)}) copy-start(f32[128,1]{0,1:T(1,128)} %get-tuple-element.578) | copy-start | bytes 1540 | tf_op jit(solution)/shard_map/while
  183.4 2.3 collective-permute-start
  189.0 17.9 %copy-start.5 = (f32[128,1]{0,1:T(1,128)S(1)}, f32[128,1]{0,1:T(1,128)}, u32[]{:S(2)}) copy-start(f32[128,1]{0,1:T(1,128)} %get-tuple-element.578) | copy-start | bytes 1540 | tf_op jit(solution)/shard_map/while
  209.3 6.2 %collective-permute-start = (bf16[16,4096]{1,0:T(8,128)(2,1)S(1)}, bf16[16,4096]{1,0:T(8,128)(2,1)S(1)}, u32[]{:S(2)}, u32[]{:S(2)}) collective-permute-start(bf16[16,4096]{1,0:T(8,128)(2,1)S(1)} %get-tuple-element.588), channel_id=1, source_target_pairs={{16,0},{17,1},{18,2},{19,3},{20,4},{21,5},{22,6},{23,7},{24,8},{25... | collective-permute-start | bytes 393224 | tf_op jit(solution)/shard_map/while/body/eval_jaxpr/ppermute | solution.py:16
  218.8 17.9 %copy-start.5 = (f32[128,1]{0,1:T(1,128)S(1)}, f32[128,1]{0,1:T(1,128)}, u32[]{:S(2)}) copy-start(f32[128,1]{0,1:T(1,128)} %get-tuple-element.578) | copy-start | bytes 1540 | tf_op jit(solution)/shard_map/while
  239.1 6.2 %collective-permute-start = (bf16[16,4096]{1,0:T(8,128)(2,1)S(1)}, bf16[16,4096]{1,0:T(8,128)(2,1)S(1)}, u32[]{:S(2)}, u32[]{:S(2)}) collective-permute-start(bf16[16,4096]{1,0:T(8,128)(2,1)S(1)} %get-tuple-element.588), channel_id=1, source_target_pairs={{16,0},{17,1},{18,2},{19,3},{20,4},{21,5},{22,6},{23,7},{24,8},{25... | collective-permute-start | bytes 393224 | tf_op jit(solution)/shard_map/while/body/eval_jaxpr/ppermute | solution.py:16
  248.5 17.9 %copy-start.5 = (f32[128,1]{0,1:T(1,128)S(1)}, f32[128,1]{0,1:T(1,128)}, u32[]{:S(2)}) copy-start(f32[128,1]{0,1:T(1,128)} %get-tuple-element.578) | copy-start | bytes 1540 | tf_op jit(solution)/shard_map/while
  268.8 6.1 %collective-permute-start = (bf16[16,4096]{1,0:T(8,128)(2,1)S(1)}, bf16[16,4096]{1,0:T(8,128)(2,1)S(1)}, u32[]{:S(2)}, u32[]{:S(2)}) collective-permute-start(bf16[16,4096]{1,0:T(8,128)(2,1)S(1)} %get-tuple-element.588), channel_id=1, source_target_pairs={{16,0},{17,1},{18,2},{19,3},{20,4},{21,5},{22,6},{23,7},{24,8},{25... | collective-permute-start | bytes 393224 | tf_op jit(solution)/shard_map/while/body/eval_jaxpr/ppermute | solution.py:16
  278.2 17.9 %copy-start.5 = (f32[128,1]{0,1:T(1,128)S(1)}, f32[128,1]{0,1:T(1,128)}, u32[]{:S(2)}) copy-start(f32[128,1]{0,1:T(1,128)} %get-tuple-element.578) | copy-start | bytes 1540 | tf_op jit(solution)/shard_map/while
  298.5 6.1 %collective-permute-start = (bf16[16,4096]{1,0:T(8,128)(2,1)S(1)}, bf16[16,4096]{1,0:T(8,128)(2,1)S(1)}, u32[]{:S(2)}, u32[]{:S(2)}) collective-permute-start(bf16[16,4096]{1,0:T(8,128)(2,1)S(1)} %get-tuple-element.588), channel_id=1, source_target_pairs={{16,0},{17,1},{18,2},{19,3},{20,4},{21,5},{22,6},{23,7},{24,8},{25... | collective-permute-start | bytes 393224 | tf_op jit(solution)/shard_map/while/body/eval_jaxpr/ppermute | solution.py:16
  308.0 17.9 %copy-start.5 = (f32[128,1]{0,1:T(1,128)S(1)}, f32[128,1]{0,1:T(1,128)}, u32[]{:S(2)}) copy-start(f32[128,1]{0,1:T(1,128)} %get-tuple-element.578) | copy-start | bytes 1540 | tf_op jit(solution)/shard_map/while
  328.3 6.1 %collective-permute-start = (bf16[16,4096]{1,0:T(8,128)(2,1)S(1)}, bf16[16,4096]{1,0:T(8,128)(2,1)S(1)}, u32[]{:S(2)}, u32[]{:S(2)}) collective-permute-start(bf16[16,4096]{1,0:T(8,128)(2,1)S(1)} %get-tuple-element.588), channel_id=1, source_target_pairs={{16,0},{17,1},{18,2},{19,3},{20,4},{21,5},{22,6},{23,7},{24,8},{25... | collective-permute-start | bytes 393224 | tf_op jit(solution)/shard_map/while/body/eval_jaxpr/ppermute | solution.py:16
  337.7 17.9 %copy-start.5 = (f32[128,1]{0,1:T(1,128)S(1)}, f32[128,1]{0,1:T(1,128)}, u32[]{:S(2)}) copy-start(f32[128,1]{0,1:T(1,128)} %get-tuple-element.578) | copy-start | bytes 1540 | tf_op jit(solution)/shard_map/while
  358.0 6.1 %collective-permute-start = (bf16[16,4096]{1,0:T(8,128)(2,1)S(1)}, bf16[16,4096]{1,0:T(8,128)(2,1)S(1)}, u32[]{:S(2)}, u32[]{:S(2)}) collective-permute-start(bf16[16,4096]{1,0:T(8,128)(2,1)S(1)} %get-tuple-element.588), channel_id=1, source_target_pairs={{16,0},{17,1},{18,2},{19,3},{20,4},{21,5},{22,6},{23,7},{24,8},{25... | collective-permute-start | bytes 393224 | tf_op jit(solution)/shard_map/while/body/eval_jaxpr/ppermute | solution.py:16
  367.4 17.9 %copy-start.5 = (f32[128,1]{0,1:T(1,128)S(1)}, f32[128,1]{0,1:T(1,128)}, u32[]{:S(2)}) copy-start(f32[128,1]{0,1:T(1,128)} %get-tuple-element.578) | copy-start | bytes 1540 | tf_op jit(solution)/shard_map/while
  387.6 6.2 %collective-permute-start = (bf16[16,4096]{1,0:T(8,128)(2,1)S(1)}, bf16[16,4096]{1,0:T(8,128)(2,1)S(1)}, u32[]{:S(2)}, u32[]{:S(2)}) collective-permute-start(bf16[16,4096]{1,0:T(8,128)(2,1)S(1)} %get-tuple-element.588), channel_id=1, source_target_pairs={{16,0},{17,1},{18,2},{19,3},{20,4},{21,5},{22,6},{23,7},{24,8},{25... | collective-permute-start | bytes 393224 | tf_op jit(solution)/shard_map/while/body/eval_jaxpr/ppermute | solution.py:16
  397.1 10.5 %copy-start.5 = (f32[128,1]{0,1:T(1,128)S(1)}, f32[128,1]{0,1:T(1,128)}, u32[]{:S(2)}) copy-start(f32[128,1]{0,1:T(1,128)} %get-tuple-element.578) | copy-start | bytes 1540 | tf_op jit(solution)/shard_map/while
  407.7 15.8 %collective-permute-start = (bf16[16,4096]{1,0:T(8,128)(2,1)S(1)}, bf16[16,4096]{1,0:T(8,128)(2,1)S(1)}, u32[]{:S(2)}, u32[]{:S(2)}) collective-permute-start(bf16[16,4096]{1,0:T(8,128)(2,1)S(1)} %get-tuple-element.588), channel_id=1, source_target_pairs={{16,0},{17,1},{18,2},{19,3},{20,4},{21,5},{22,6},{23,7},{24,8},{25... | collective-permute-start | bytes 393224 | tf_op jit(solution)/shard_map/while/body/eval_jaxpr/ppermute | solution.py:16
  432.8 18.3 %copy-start.3 = (f32[2,1024]{1,0:T(2,128)}, f32[2,1024]{1,0:T(2,128)S(1)}, u32[]{:S(2)}) copy-start(f32[2,1024]{1,0:T(2,128)S(1)} %psum.22) | copy-start | bytes 24580
Sparse Core Ops, SparseCore 0:
  9.9 89.3 all-gather.2
  105.1 52.1 all-reduce.1
where the time goes:
time: 461 us; the launch traced here: 458 us
  waiting for transfers between devices  143 us (31%)
  blocking collectives  120 us (26%)
  matrix products  67.3 us (15%)
  other arithmetic  54.6 us (12%)
  starting transfers between devices  52.6 us (11%)
  between operations  15.4 us (3%)
    all_gather x9, blocking collectives, turn(): full_grads = lax.all_gather(own_grads, 'tensor', axis=1, tiled=True)  94.2 us
    all_gather x1, waiting for transfers between devices, body(): weight_rows = lax.all_gather(weights[0], 'dp', axis=1, tiled=True)  88.2 us
    ppermute x9, starting transfers between devices, passed_along(): lax.ppermute(value, axis, [(source, source + steps) for source in range(f...  52.5 us
    psum x1, waiting for transfers between devices, body(): lax.psum(partial_value.astype(jnp.bfloat16), 'tensor').astype(jnp.float32)  45.8 us
    dot_general x8, matrix products, block_grad(): lax.dot_general(grad_pre, weight_rows, (((1,), (1,)), ((), ())), preferre...  45.2 us
    convert_element_type x9, other arithmetic, sign_table(): (jnp.where(parity == 1, 1.0, -1.0) * (1.0 / math.sqrt(row_count))).astype...  21 us
    psum x1, blocking collectives, body(): scores = lax.psum(partial_scores, ('section', 'tensor'))  18.1 us
    dot_general x8, matrix products, block_grad(): lax.dot_general(feature_rows, out_features, (((0,), (0,)), ((), ())), pre...  14.2 us
  transfers between devices with their start and end apart: 11, of which 11 were waited for; matrix products, arithmetic and copies ran while one was open for 2% of the time, Pallas kernels for 0%

commit v1 on v0

--- a/solution.py
+++ b/solution.py
@@ -49,7 +49,7 @@
     radius = jnp.sqrt(jnp.mean(hidden_in * hidden_in, axis=1, keepdims=True) + eps)
     normed = hidden_in / radius
     lifted = (normed * gain_row).astype(jnp.bfloat16)
-    weight_rows = lax.all_gather(weights[0], "dp", axis=1, tiled=True)
+    weight_rows = jnp.concatenate(lax.all_gather(weights[0], "dp"), axis=1)
     lifted_own = lax.dynamic_slice_in_dim(lifted, own_start, slice_width, 1)
     partial_value = jnp.dot(lifted_own, weight_rows, preferred_element_type=jnp.float32)
     summed = lax.psum(partial_value.astype(jnp.bfloat16), "tensor").astype(jnp.float32)

time: 461 us -> 475 us (1.030)
  local copies, waits for them, and re-layouts: 3.93 us -> 26.8 us
  waiting for transfers between devices: 143 us -> 132 us
    all_gather x0 -> x1, local copies, waits for them, and re-layouts: none -> 11.4 us  [body(): weight_rows = jnp.concatenate(lax.all_gather(weights[0], 'dp'), axis=1)]
    unnamed x11 -> x12, local copies, waits for them, and re-layouts: 1.2 us -> 12.6 us
    psum x1, waiting for transfers between devices: 45.8 us -> 34.5 us  [body(): lax.psum(partial_value.astype(jnp.bfloat16), 'tensor').astype(jnp.float32)]
  transfers between devices with their start and end apart: 11 -> 11, of which waited for: 11 -> 11; matrix products, arithmetic and copies ran while one was open for 2% -> 4% of each run, Pallas kernels for 0% -> 0%
where the time goes in v1:
time: 475 us; the launch traced here: 471 us
  waiting for transfers between devices  132 us (28%)
  blocking collectives  120 us (25%)
  matrix products  69 us (15%)
  other arithmetic  54.8 us (12%)
  starting transfers between devices  52.6 us (11%)
  local copies, waits for them, and re-layouts  26.8 us (6%)
  between operations  15.4 us (3%)
    all_gather x9, blocking collectives, turn(): full_grads = lax.all_gather(own_grads, 'tensor', axis=1, tiled=True)  94.2 us
    all_gather x1, waiting for transfers between devices, body(): weight_rows = jnp.concatenate(lax.all_gather(weights[0], 'dp'), axis=1)  88.2 us
    ppermute x9, starting transfers between devices, passed_along(): lax.ppermute(value, axis, [(source, source + steps) for source in range(f...  52.5 us
    dot_general x8, matrix products, block_grad(): lax.dot_general(grad_pre, weight_rows, (((1,), (1,)), ((), ())), preferre...  45.2 us
    psum x1, waiting for transfers between devices, body(): lax.psum(partial_value.astype(jnp.bfloat16), 'tensor').astype(jnp.float32)  34.5 us
    convert_element_type x9, other arithmetic, sign_table(): (jnp.where(parity == 1, 1.0, -1.0) * (1.0 / math.sqrt(row_count))).astype...  21.1 us
    psum x1, blocking collectives, body(): scores = lax.psum(partial_scores, ('section', 'tensor'))  18.1 us
    dot_general x8, matrix products, block_grad(): lax.dot_general(feature_rows, out_features, (((0,), (0,)), ((), ())), pre...  14.2 us
  transfers between devices with their start and end apart: 11, of which 11 were waited for; matrix products, arithmetic and copies ran while one was open for 4% of the time, Pallas kernels for 0%

profile of v1, /device:TPU:1, one launch (start us, length us, event | category | flops | bytes accessed | tf_op | source)
XLA Modules:
  0.0 471.1 jit_solution(14049588950372934262)
XLA Ops:
  11.1 88.2 %all-gather.2.cloned.1.call-done = bf16[4,1024,1024]{2,1,0:T(8,128)(2,1)} async-done(((bf16[1,1024,1024]{2,1,0:T(8,128)(2,1)}), bf16[4,1024,1024]{2,1,0:T(8,128)(2,1)}) %all-gather.2.cloned.1.call-update) | async-done | bytes 8388624 | tf_op jit(solution)/shard_map/all_gather | solution.py:52
  99.3 11.4 %copy.11 = bf16[4,1024,1024]{1,2,0:T(8,128)(2,1)} copy(bf16[4,1024,1024]{2,1,0:T(8,128)(2,1)} %all-gather.2.cloned.1.call-done) | data formatting | bytes 16777216 | tf_op jit(solution)/shard_map/all_gather | solution.py:52
  110.7 7.3 %convolution_convert_fusion.2 = bf16[128,4096]{1,0:T(8,128)(2,1)} fusion(bf16[1024,4096]{0,1:T(8,128)(2,1)} %bitcast.26, bf16[128,4096]{1,0:T(8,128)(2,1)S(1)} %get-tuple-element.451, s32[]{:T(128)S(6)} %select_n.44), kind=kOutput, calls=%fused_computation.21 | convolution fusion | flops 1074266112 | bytes 9699332 | tf_op jit(solution)/shard_map/dot_general | solution.py:54
  121.0 2.1 convolution_convert_fusion.3
  124.4 11.4 %copy.12 = bf16[1024,4096]{1,0:T(8,128)(2,1)} copy(bf16[1024,4096]{0,1:T(8,128)(2,1)} %bitcast.27) | data formatting | bytes 16777216
  135.8 34.5 %all-reduce.2.cloned.1.call-done = bf16[128,4096]{1,0:T(8,128)(2,1)} async-done(((bf16[128,4096]{1,0:T(8,128)(2,1)}), bf16[128,4096]{1,0:T(8,128)(2,1)}) %all-reduce.2.cloned.1.call-update) | async-done | bytes 1048592 | tf_op jit(solution)/shard_map/psum | solution.py:55
  170.3 1.9 fusion.13
  172.9 263.8 %while.19 = (s32[]{:T(128)}, bf16[16,4096]{1,0:T(8,128)(2,1)S(1)}, f32[64,64]{1,0:T(8,128)}, s32[]{:T(128)}, pred[]{:T(512)}, /*index=5*/bf16[128,4096]{1,0:T(8,...) while((s32[]{:T(128)}, bf16[16,4096]{1,0:T(8,128)(2,1)S(1)}, ...), condition=%wide.region_8.9_spmd.clone, body=%wide.region_2.8_spmd.clone.sunk | while | flops 147674128 | bytes 13017286 | solution.py:121
  172.9 2.4 multiply_convert_fusion.9
  176.2 7.5 %conditional.6 = (bf16[16,1024]{1,0:T(8,128)(2,1)S(1)}, f32[64,64]{1,0:T(8,128)}) conditional(s32[]{:T(128)} %convert_element_type.134, f32[64,64]{1,0:T(8,128)} %get-tuple-element.578, (bf16[16,4096]{1,0:T(8,128)(2,1)S(1)}, f32[128,4096]{1,0:T(8,128)S(1)}, s32[]{:T(128)}, bf16[1024,4096]{1,0:T(8,128)(2,1)}, bf16[128,64]{1,0:T(8,128)(2,1)}, ...), branch_computations={%region_3.3_spmd, %region_4.4_spmd} | conditional | flops 143152128 | bytes 10310676 | solution.py:92
  176.3 5.6 %convolution_convert_fusion = bf16[16,1024]{1,0:T(8,128)(2,1)S(1)} fusion(bf16[1024,4096]{1,0:T(8,128)(2,1)} %get-tuple-element.308, f32[128,4096]{1,0:T(8,128)S(1)} %get-tuple-element.306, s32[]{:T(128)} %get-tuple-element.307, bf16[16,4096]{1,0:T(8,128)(2,1)S(1)} %get-tuple-element.305), kind=kOutput, calls=%fused_computation.1 | convolution fusion | flops 134430720 | bytes 8814596 | tf_op jit(solution)/shard_map/while/body/eval_jaxpr/cond/branch_1_fun/dot_general | solution.py:73
  181.9 1.8 convolution_add_fusion
  183.7 10.4 %all_gather.13 = bf16[16,4096]{1,0:T(8,128)(2,1)S(1)} all-gather(bf16[16,1024]{1,0:T(8,128)(2,1)S(1)} %get-tuple-element.549), channel_id=1, replica_groups=mesh['section'=2,'dp'=4,'tensor'=4] {'tensor'}, dimensions={1}, use_global_device_ids=true | all-gather | bytes 163840 | tf_op jit(solution)/shard_map/while/body/eval_jaxpr/all_gather | solution.py:98
  194.1 2.4 conditional.7
  198.8 2.3 multiply_convert_fusion.9
  202.1 7.5 %conditional.6 = (bf16[16,1024]{1,0:T(8,128)(2,1)S(1)}, f32[64,64]{1,0:T(8,128)}) conditional(s32[]{:T(128)} %convert_element_type.134, f32[64,64]{1,0:T(8,128)} %get-tuple-element.578, (bf16[16,4096]{1,0:T(8,128)(2,1)S(1)}, f32[128,4096]{1,0:T(8,128)S(1)}, s32[]{:T(128)}, bf16[1024,4096]{1,0:T(8,128)(2,1)}, bf16[128,64]{1,0:T(8,128)(2,1)}, ...), branch_computations={%region_3.3_spmd, %region_4.4_spmd} | conditional | flops 143152128 | bytes 10310676 | solution.py:92
  202.1 5.6 %convolution_convert_fusion = bf16[16,1024]{1,0:T(8,128)(2,1)S(1)} fusion(bf16[1024,4096]{1,0:T(8,128)(2,1)} %get-tuple-element.308, f32[128,4096]{1,0:T(8,128)S(1)} %get-tuple-element.306, s32[]{:T(128)} %get-tuple-element.307, bf16[16,4096]{1,0:T(8,128)(2,1)S(1)} %get-tuple-element.305), kind=kOutput, calls=%fused_computation.1 | convolution fusion | flops 134430720 | bytes 8814596 | tf_op jit(solution)/shard_map/while/body/eval_jaxpr/cond/branch_1_fun/dot_general | solution.py:73
  207.7 1.8 convolution_add_fusion
  209.5 10.5 %all_gather.13 = bf16[16,4096]{1,0:T(8,128)(2,1)S(1)} all-gather(bf16[16,1024]{1,0:T(8,128)(2,1)S(1)} %get-tuple-element.549), channel_id=1, replica_groups=mesh['section'=2,'dp'=4,'tensor'=4] {'tensor'}, dimensions={1}, use_global_device_ids=true | all-gather | bytes 163840 | tf_op jit(solution)/shard_map/while/body/eval_jaxpr/all_gather | solution.py:98
  220.0 2.4 conditional.7
  222.4 5.2 %collective-permute-start = (bf16[16,4096]{1,0:T(8,128)(2,1)S(1)}, bf16[16,4096]{1,0:T(8,128)(2,1)S(1)}, u32[]{:S(2)}, u32[]{:S(2)}) collective-permute-start(bf16[16,4096]{1,0:T(8,128)(2,1)S(1)} %get-tuple-element.618), channel_id=1, source_target_pairs={{16,0},{17,1},{18,2},{19,3},{20,4},{21,5},{22,6},{23,7},{24,8},{25... | collective-permute-start | bytes 393224 | tf_op jit(solution)/shard_map/while/body/eval_jaxpr/ppermute | solution.py:16
  228.6 2.3 multiply_convert_fusion.9
  231.9 7.5 %conditional.6 = (bf16[16,1024]{1,0:T(8,128)(2,1)S(1)}, f32[64,64]{1,0:T(8,128)}) conditional(s32[]{:T(128)} %convert_element_type.134, f32[64,64]{1,0:T(8,128)} %get-tuple-element.578, (bf16[16,4096]{1,0:T(8,128)(2,1)S(1)}, f32[128,4096]{1,0:T(8,128)S(1)}, s32[]{:T(128)}, bf16[1024,4096]{1,0:T(8,128)(2,1)}, bf16[128,64]{1,0:T(8,128)(2,1)}, ...), branch_computations={%region_3.3_spmd, %region_4.4_spmd} | conditional | flops 143152128 | bytes 10310676 | solution.py:92
  231.9 5.6 %convolution_convert_fusion = bf16[16,1024]{1,0:T(8,128)(2,1)S(1)} fusion(bf16[1024,4096]{1,0:T(8,128)(2,1)} %get-tuple-element.308, f32[128,4096]{1,0:T(8,128)S(1)} %get-tuple-element.306, s32[]{:T(128)} %get-tuple-element.307, bf16[16,4096]{1,0:T(8,128)(2,1)S(1)} %get-tuple-element.305), kind=kOutput, calls=%fused_computation.1 | convolution fusion | flops 134430720 | bytes 8814596 | tf_op jit(solution)/shard_map/while/body/eval_jaxpr/cond/branch_1_fun/dot_general | solution.py:73
  239.3 10.5 %all_gather.13 = bf16[16,4096]{1,0:T(8,128)(2,1)S(1)} all-gather(bf16[16,1024]{1,0:T(8,128)(2,1)S(1)} %get-tuple-element.549), channel_id=1, replica_groups=mesh['section'=2,'dp'=4,'tensor'=4] {'tensor'}, dimensions={1}, use_global_device_ids=true | all-gather | bytes 163840 | tf_op jit(solution)/shard_map/while/body/eval_jaxpr/all_gather | solution.py:98
  249.8 2.4 conditional.7
  252.2 5.2 %collective-permute-start = (bf16[16,4096]{1,0:T(8,128)(2,1)S(1)}, bf16[16,4096]{1,0:T(8,128)(2,1)S(1)}, u32[]{:S(2)}, u32[]{:S(2)}) collective-permute-start(bf16[16,4096]{1,0:T(8,128)(2,1)S(1)} %get-tuple-element.618), channel_id=1, source_target_pairs={{16,0},{17,1},{18,2},{19,3},{20,4},{21,5},{22,6},{23,7},{24,8},{25... | collective-permute-start | bytes 393224 | tf_op jit(solution)/shard_map/while/body/eval_jaxpr/ppermute | solution.py:16
  258.3 2.3 multiply_convert_fusion.9
  261.6 7.5 %conditional.6 = (bf16[16,1024]{1,0:T(8,128)(2,1)S(1)}, f32[64,64]{1,0:T(8,128)}) conditional(s32[]{:T(128)} %convert_element_type.134, f32[64,64]{1,0:T(8,128)} %get-tuple-element.578, (bf16[16,4096]{1,0:T(8,128)(2,1)S(1)}, f32[128,4096]{1,0:T(8,128)S(1)}, s32[]{:T(128)}, bf16[1024,4096]{1,0:T(8,128)(2,1)}, bf16[128,64]{1,0:T(8,128)(2,1)}, ...), branch_computations={%region_3.3_spmd, %region_4.4_spmd} | conditional | flops 143152128 | bytes 10310676 | solution.py:92
  261.7 5.6 %convolution_convert_fusion = bf16[16,1024]{1,0:T(8,128)(2,1)S(1)} fusion(bf16[1024,4096]{1,0:T(8,128)(2,1)} %get-tuple-element.308, f32[128,4096]{1,0:T(8,128)S(1)} %get-tuple-element.306, s32[]{:T(128)} %get-tuple-element.307, bf16[16,4096]{1,0:T(8,128)(2,1)S(1)} %get-tuple-element.305), kind=kOutput, calls=%fused_computation.1 | convolution fusion | flops 134430720 | bytes 8814596 | tf_op jit(solution)/shard_map/while/body/eval_jaxpr/cond/branch_1_fun/dot_general | solution.py:73
  267.3 1.8 convolution_add_fusion
  269.1 10.5 %all_gather.13 = bf16[16,4096]{1,0:T(8,128)(2,1)S(1)} all-gather(bf16[16,1024]{1,0:T(8,128)(2,1)S(1)} %get-tuple-element.549), channel_id=1, replica_groups=mesh['section'=2,'dp'=4,'tensor'=4] {'tensor'}, dimensions={1}, use_global_device_ids=true | all-gather | bytes 163840 | tf_op jit(solution)/shard_map/while/body/eval_jaxpr/all_gather | solution.py:98
  279.6 2.4 conditional.7
  281.9 5.2 %collective-permute-start = (bf16[16,4096]{1,0:T(8,128)(2,1)S(1)}, bf16[16,4096]{1,0:T(8,128)(2,1)S(1)}, u32[]{:S(2)}, u32[]{:S(2)}) collective-permute-start(bf16[16,4096]{1,0:T(8,128)(2,1)S(1)} %get-tuple-element.618), channel_id=1, source_target_pairs={{16,0},{17,1},{18,2},{19,3},{20,4},{21,5},{22,6},{23,7},{24,8},{25... | collective-permute-start | bytes 393224 | tf_op jit(solution)/shard_map/while/body/eval_jaxpr/ppermute | solution.py:16
  288.1 2.3 multiply_convert_fusion.9
  291.4 7.5 %conditional.6 = (bf16[16,1024]{1,0:T(8,128)(2,1)S(1)}, f32[64,64]{1,0:T(8,128)}) conditional(s32[]{:T(128)} %convert_element_type.134, f32[64,64]{1,0:T(8,128)} %get-tuple-element.578, (bf16[16,4096]{1,0:T(8,128)(2,1)S(1)}, f32[128,4096]{1,0:T(8,128)S(1)}, s32[]{:T(128)}, bf16[1024,4096]{1,0:T(8,128)(2,1)}, bf16[128,64]{1,0:T(8,128)(2,1)}, ...), branch_computations={%region_3.3_spmd, %region_4.4_spmd} | conditional | flops 143152128 | bytes 10310676 | solution.py:92
  291.4 5.6 %convolution_convert_fusion = bf16[16,1024]{1,0:T(8,128)(2,1)S(1)} fusion(bf16[1024,4096]{1,0:T(8,128)(2,1)} %get-tuple-element.308, f32[128,4096]{1,0:T(8,128)S(1)} %get-tuple-element.306, s32[]{:T(128)} %get-tuple-element.307, bf16[16,4096]{1,0:T(8,128)(2,1)S(1)} %get-tuple-element.305), kind=kOutput, calls=%fused_computation.1 | convolution fusion | flops 134430720 | bytes 8814596 | tf_op jit(solution)/shard_map/while/body/eval_jaxpr/cond/branch_1_fun/dot_general | solution.py:73
  297.0 1.8 convolution_add_fusion
  298.8 10.5 %all_gather.13 = bf16[16,4096]{1,0:T(8,128)(2,1)S(1)} all-gather(bf16[16,1024]{1,0:T(8,128)(2,1)S(1)} %get-tuple-element.549), channel_id=1, replica_groups=mesh['section'=2,'dp'=4,'tensor'=4] {'tensor'}, dimensions={1}, use_global_device_ids=true | all-gather | bytes 163840 | tf_op jit(solution)/shard_map/while/body/eval_jaxpr/all_gather | solution.py:98
  309.3 2.4 conditional.7
  311.7 5.2 %collective-permute-start = (bf16[16,4096]{1,0:T(8,128)(2,1)S(1)}, bf16[16,4096]{1,0:T(8,128)(2,1)S(1)}, u32[]{:S(2)}, u32[]{:S(2)}) collective-permute-start(bf16[16,4096]{1,0:T(8,128)(2,1)S(1)} %get-tuple-element.618), channel_id=1, source_target_pairs={{16,0},{17,1},{18,2},{19,3},{20,4},{21,5},{22,6},{23,7},{24,8},{25... | collective-permute-start | bytes 393224 | tf_op jit(solution)/shard_map/while/body/eval_jaxpr/ppermute | solution.py:16
  317.8 2.3 multiply_convert_fusion.9
  321.1 7.5 %conditional.6 = (bf16[16,1024]{1,0:T(8,128)(2,1)S(1)}, f32[64,64]{1,0:T(8,128)}) conditional(s32[]{:T(128)} %convert_element_type.134, f32[64,64]{1,0:T(8,128)} %get-tuple-element.578, (bf16[16,4096]{1,0:T(8,128)(2,1)S(1)}, f32[128,4096]{1,0:T(8,128)S(1)}, s32[]{:T(128)}, bf16[1024,4096]{1,0:T(8,128)(2,1)}, bf16[128,64]{1,0:T(8,128)(2,1)}, ...), branch_computations={%region_3.3_spmd, %region_4.4_spmd} | conditional | flops 143152128 | bytes 10310676 | solution.py:92
  321.1 5.6 %convolution_convert_fusion = bf16[16,1024]{1,0:T(8,128)(2,1)S(1)} fusion(bf16[1024,4096]{1,0:T(8,128)(2,1)} %get-tuple-element.308, f32[128,4096]{1,0:T(8,128)S(1)} %get-tuple-element.306, s32[]{:T(128)} %get-tuple-element.307, bf16[16,4096]{1,0:T(8,128)(2,1)S(1)} %get-tuple-element.305), kind=kOutput, calls=%fused_computation.1 | convolution fusion | flops 134430720 | bytes 8814596 | tf_op jit(solution)/shard_map/while/body/eval_jaxpr/cond/branch_1_fun/dot_general | solution.py:73
  328.6 10.5 %all_gather.13 = bf16[16,4096]{1,0:T(8,128)(2,1)S(1)} all-gather(bf16[16,1024]{1,0:T(8,128)(2,1)S(1)} %get-tuple-element.549), channel_id=1, replica_groups=mesh['section'=2,'dp'=4,'tensor'=4] {'tensor'}, dimensions={1}, use_global_device_ids=true | all-gather | bytes 163840 | tf_op jit(solution)/shard_map/while/body/eval_jaxpr/all_gather | solution.py:98
  339.0 2.4 conditional.7
  341.4 5.2 %collective-permute-start = (bf16[16,4096]{1,0:T(8,128)(2,1)S(1)}, bf16[16,4096]{1,0:T(8,128)(2,1)S(1)}, u32[]{:S(2)}, u32[]{:S(2)}) collective-permute-start(bf16[16,4096]{1,0:T(8,128)(2,1)S(1)} %get-tuple-element.618), channel_id=1, source_target_pairs={{16,0},{17,1},{18,2},{19,3},{20,4},{21,5},{22,6},{23,7},{24,8},{25... | collective-permute-start | bytes 393224 | tf_op jit(solution)/shard_map/while/body/eval_jaxpr/ppermute | solution.py:16
  347.6 2.3 multiply_convert_fusion.9
  350.9 7.5 %conditional.6 = (bf16[16,1024]{1,0:T(8,128)(2,1)S(1)}, f32[64,64]{1,0:T(8,128)}) conditional(s32[]{:T(128)} %convert_element_type.134, f32[64,64]{1,0:T(8,128)} %get-tuple-element.578, (bf16[16,4096]{1,0:T(8,128)(2,1)S(1)}, f32[128,4096]{1,0:T(8,128)S(1)}, s32[]{:T(128)}, bf16[1024,4096]{1,0:T(8,128)(2,1)}, bf16[128,64]{1,0:T(8,128)(2,1)}, ...), branch_computations={%region_3.3_spmd, %region_4.4_spmd} | conditional | flops 143152128 | bytes 10310676 | solution.py:92
  350.9 5.6 %convolution_convert_fusion = bf16[16,1024]{1,0:T(8,128)(2,1)S(1)} fusion(bf16[1024,4096]{1,0:T(8,128)(2,1)} %get-tuple-element.308, f32[128,4096]{1,0:T(8,128)S(1)} %get-tuple-element.306, s32[]{:T(128)} %get-tuple-element.307, bf16[16,4096]{1,0:T(8,128)(2,1)S(1)} %get-tuple-element.305), kind=kOutput, calls=%fused_computation.1 | convolution fusion | flops 134430720 | bytes 8814596 | tf_op jit(solution)/shard_map/while/body/eval_jaxpr/cond/branch_1_fun/dot_general | solution.py:73
  358.3 10.5 %all_gather.13 = bf16[16,4096]{1,0:T(8,128)(2,1)S(1)} all-gather(bf16[16,1024]{1,0:T(8,128)(2,1)S(1)} %get-tuple-element.549), channel_id=1, replica_groups=mesh['section'=2,'dp'=4,'tensor'=4] {'tensor'}, dimensions={1}, use_global_device_ids=true | all-gather | bytes 163840 | tf_op jit(solution)/shard_map/while/body/eval_jaxpr/all_gather | solution.py:98
  368.8 2.4 conditional.7
  371.2 5.2 %collective-permute-start = (bf16[16,4096]{1,0:T(8,128)(2,1)S(1)}, bf16[16,4096]{1,0:T(8,128)(2,1)S(1)}, u32[]{:S(2)}, u32[]{:S(2)}) collective-permute-start(bf16[16,4096]{1,0:T(8,128)(2,1)S(1)} %get-tuple-element.618), channel_id=1, source_target_pairs={{16,0},{17,1},{18,2},{19,3},{20,4},{21,5},{22,6},{23,7},{24,8},{25... | collective-permute-start | bytes 393224 | tf_op jit(solution)/shard_map/while/body/eval_jaxpr/ppermute | solution.py:16
  377.3 2.3 multiply_convert_fusion.9
  380.6 7.4 %conditional.6 = (bf16[16,1024]{1,0:T(8,128)(2,1)S(1)}, f32[64,64]{1,0:T(8,128)}) conditional(s32[]{:T(128)} %convert_element_type.134, f32[64,64]{1,0:T(8,128)} %get-tuple-element.578, (bf16[16,4096]{1,0:T(8,128)(2,1)S(1)}, f32[128,4096]{1,0:T(8,128)S(1)}, s32[]{:T(128)}, bf16[1024,4096]{1,0:T(8,128)(2,1)}, bf16[128,64]{1,0:T(8,128)(2,1)}, ...), branch_computations={%region_3.3_spmd, %region_4.4_spmd} | conditional | flops 143152128 | bytes 10310676 | solution.py:92
  380.6 5.6 %convolution_convert_fusion = bf16[16,1024]{1,0:T(8,128)(2,1)S(1)} fusion(bf16[1024,4096]{1,0:T(8,128)(2,1)} %get-tuple-element.308, f32[128,4096]{1,0:T(8,128)S(1)} %get-tuple-element.306, s32[]{:T(128)} %get-tuple-element.307, bf16[16,4096]{1,0:T(8,128)(2,1)S(1)} %get-tuple-element.305), kind=kOutput, calls=%fused_computation.1 | convolution fusion | flops 134430720 | bytes 8814596 | tf_op jit(solution)/shard_map/while/body/eval_jaxpr/cond/branch_1_fun/dot_general | solution.py:73
  388.0 10.5 %all_gather.13 = bf16[16,4096]{1,0:T(8,128)(2,1)S(1)} all-gather(bf16[16,1024]{1,0:T(8,128)(2,1)S(1)} %get-tuple-element.549), channel_id=1, replica_groups=mesh['section'=2,'dp'=4,'tensor'=4] {'tensor'}, dimensions={1}, use_global_device_ids=true | all-gather | bytes 163840 | tf_op jit(solution)/shard_map/while/body/eval_jaxpr/all_gather | solution.py:98
  398.5 2.3 conditional.7
  400.8 5.3 %collective-permute-start = (bf16[16,4096]{1,0:T(8,128)(2,1)S(1)}, bf16[16,4096]{1,0:T(8,128)(2,1)S(1)}, u32[]{:S(2)}, u32[]{:S(2)}) collective-permute-start(bf16[16,4096]{1,0:T(8,128)(2,1)S(1)} %get-tuple-element.618), channel_id=1, source_target_pairs={{16,0},{17,1},{18,2},{19,3},{20,4},{21,5},{22,6},{23,7},{24,8},{25... | collective-permute-start | bytes 393224 | tf_op jit(solution)/shard_map/while/body/eval_jaxpr/ppermute | solution.py:16
  407.0 2.3 multiply_convert_fusion.9
  410.4 10.5 %all_gather.13 = bf16[16,4096]{1,0:T(8,128)(2,1)S(1)} all-gather(bf16[16,1024]{1,0:T(8,128)(2,1)S(1)} %get-tuple-element.549), channel_id=1, replica_groups=mesh['section'=2,'dp'=4,'tensor'=4] {'tensor'}, dimensions={1}, use_global_device_ids=true | all-gather | bytes 163840 | tf_op jit(solution)/shard_map/while/body/eval_jaxpr/all_gather | solution.py:98
  420.9 14.8 %collective-permute-start = (bf16[16,4096]{1,0:T(8,128)(2,1)S(1)}, bf16[16,4096]{1,0:T(8,128)(2,1)S(1)}, u32[]{:S(2)}, u32[]{:S(2)}) collective-permute-start(bf16[16,4096]{1,0:T(8,128)(2,1)S(1)} %get-tuple-element.618), channel_id=1, source_target_pairs={{16,0},{17,1},{18,2},{19,3},{20,4},{21,5},{22,6},{23,7},{24,8},{25... | collective-permute-start | bytes 393224 | tf_op jit(solution)/shard_map/while/body/eval_jaxpr/ppermute | solution.py:16
  438.2 7.8 %psum.22 = f32[2,1024]{1,0:T(2,128)S(1)} all-reduce(f32[2,1024]{1,0:T(2,128)S(1)} %broadcast_multiply_fusion.1), channel_id=1, replica_groups=mesh['section'=2,'dp'=4,'tensor'=4] {'dp'}, use_global_device_ids=true, to_apply=%region_9.10 | all-reduce | flops 2048 | bytes 16384 | tf_op jit(solution)/shard_map/psum | solution.py:128
  446.2 18.1 %psum.23 = f32[2,64]{1,0:T(2,128)} all-reduce(f32[2,64]{1,0:T(2,128)S(1)} %fusion.32), channel_id=1, replica_groups=mesh['section'=2,'dp'=4,'tensor'=4] {'section','tensor'}, use_global_device_ids=true, to_apply=%region_10.11 | all-reduce | flops 128 | bytes 1024 | tf_op jit(solution)/shard_map/psum | solution.py:131
  (105 shorter events, 53.7 us)
Async XLA Ops:
  7.2 438.9 %copy-start = (bf16[1,64,1024]{2,1,0:T(8,128)(2,1)S(1)}, bf16[1,64,1024]{2,1,0:T(8,128)(2,1)}, u32[]{:S(2)}) copy-start(bf16[1,64,1024]{2,1,0:T(8,128)(2,1)} %param.17) | copy-start | bytes 393220
  7.2 1.3 copy-start.1
  7.2 2.1 copy-start.2
  7.2 92.1 %all-gather.2.cloned.1.call-start = ((), (), s32[]{:S(2)}) async-start(), calls=%async_computation | async-start | bytes 10485760 | tf_op jit(solution)/shard_map/all_gather | solution.py:52
  7.9 162.4 %all-reduce.2.cloned.1.call-start = ((), (), s32[]{:S(2)}) async-start(), calls=%async_computation.1 | async-start | bytes 2097152 | tf_op jit(solution)/shard_map/psum | solution.py:55
  110.7 7.3 %copy-start.4 = (s32[1,2]{1,0:T(1,128)S(1)}, s32[1,2]{1,0:T(1,128)}, u32[]{:S(2)}) copy-start(s32[1,2]{1,0:T(1,128)} %param.15) | copy-start | bytes 28
  176.2 17.9 %copy-start.5 = (f32[128,1]{0,1:T(1,128)S(1)}, f32[128,1]{0,1:T(1,128)}, u32[]{:S(2)}) copy-start(f32[128,1]{0,1:T(1,128)} %get-tuple-element.608) | copy-start | bytes 1540 | tf_op jit(solution)/shard_map/while
  196.5 2.3 collective-permute-start
  202.1 17.9 %copy-start.5 = (f32[128,1]{0,1:T(1,128)S(1)}, f32[128,1]{0,1:T(1,128)}, u32[]{:S(2)}) copy-start(f32[128,1]{0,1:T(1,128)} %get-tuple-element.608) | copy-start | bytes 1540 | tf_op jit(solution)/shard_map/while
  222.4 6.2 %collective-permute-start = (bf16[16,4096]{1,0:T(8,128)(2,1)S(1)}, bf16[16,4096]{1,0:T(8,128)(2,1)S(1)}, u32[]{:S(2)}, u32[]{:S(2)}) collective-permute-start(bf16[16,4096]{1,0:T(8,128)(2,1)S(1)} %get-tuple-element.618), channel_id=1, source_target_pairs={{16,0},{17,1},{18,2},{19,3},{20,4},{21,5},{22,6},{23,7},{24,8},{25... | collective-permute-start | bytes 393224 | tf_op jit(solution)/shard_map/while/body/eval_jaxpr/ppermute | solution.py:16
  231.9 17.9 %copy-start.5 = (f32[128,1]{0,1:T(1,128)S(1)}, f32[128,1]{0,1:T(1,128)}, u32[]{:S(2)}) copy-start(f32[128,1]{0,1:T(1,128)} %get-tuple-element.608) | copy-start | bytes 1540 | tf_op jit(solution)/shard_map/while
  252.2 6.2 %collective-permute-start = (bf16[16,4096]{1,0:T(8,128)(2,1)S(1)}, bf16[16,4096]{1,0:T(8,128)(2,1)S(1)}, u32[]{:S(2)}, u32[]{:S(2)}) collective-permute-start(bf16[16,4096]{1,0:T(8,128)(2,1)S(1)} %get-tuple-element.618), channel_id=1, source_target_pairs={{16,0},{17,1},{18,2},{19,3},{20,4},{21,5},{22,6},{23,7},{24,8},{25... | collective-permute-start | bytes 393224 | tf_op jit(solution)/shard_map/while/body/eval_jaxpr/ppermute | solution.py:16
  261.6 17.9 %copy-start.5 = (f32[128,1]{0,1:T(1,128)S(1)}, f32[128,1]{0,1:T(1,128)}, u32[]{:S(2)}) copy-start(f32[128,1]{0,1:T(1,128)} %get-tuple-element.608) | copy-start | bytes 1540 | tf_op jit(solution)/shard_map/while
  281.9 6.1 %collective-permute-start = (bf16[16,4096]{1,0:T(8,128)(2,1)S(1)}, bf16[16,4096]{1,0:T(8,128)(2,1)S(1)}, u32[]{:S(2)}, u32[]{:S(2)}) collective-permute-start(bf16[16,4096]{1,0:T(8,128)(2,1)S(1)} %get-tuple-element.618), channel_id=1, source_target_pairs={{16,0},{17,1},{18,2},{19,3},{20,4},{21,5},{22,6},{23,7},{24,8},{25... | collective-permute-start | bytes 393224 | tf_op jit(solution)/shard_map/while/body/eval_jaxpr/ppermute | solution.py:16
  291.4 17.9 %copy-start.5 = (f32[128,1]{0,1:T(1,128)S(1)}, f32[128,1]{0,1:T(1,128)}, u32[]{:S(2)}) copy-start(f32[128,1]{0,1:T(1,128)} %get-tuple-element.608) | copy-start | bytes 1540 | tf_op jit(solution)/shard_map/while
  311.7 6.1 %collective-permute-start = (bf16[16,4096]{1,0:T(8,128)(2,1)S(1)}, bf16[16,4096]{1,0:T(8,128)(2,1)S(1)}, u32[]{:S(2)}, u32[]{:S(2)}) collective-permute-start(bf16[16,4096]{1,0:T(8,128)(2,1)S(1)} %get-tuple-element.618), channel_id=1, source_target_pairs={{16,0},{17,1},{18,2},{19,3},{20,4},{21,5},{22,6},{23,7},{24,8},{25... | collective-permute-start | bytes 393224 | tf_op jit(solution)/shard_map/while/body/eval_jaxpr/ppermute | solution.py:16
  321.1 17.9 %copy-start.5 = (f32[128,1]{0,1:T(1,128)S(1)}, f32[128,1]{0,1:T(1,128)}, u32[]{:S(2)}) copy-start(f32[128,1]{0,1:T(1,128)} %get-tuple-element.608) | copy-start | bytes 1540 | tf_op jit(solution)/shard_map/while
  341.4 6.1 %collective-permute-start = (bf16[16,4096]{1,0:T(8,128)(2,1)S(1)}, bf16[16,4096]{1,0:T(8,128)(2,1)S(1)}, u32[]{:S(2)}, u32[]{:S(2)}) collective-permute-start(bf16[16,4096]{1,0:T(8,128)(2,1)S(1)} %get-tuple-element.618), channel_id=1, source_target_pairs={{16,0},{17,1},{18,2},{19,3},{20,4},{21,5},{22,6},{23,7},{24,8},{25... | collective-permute-start | bytes 393224 | tf_op jit(solution)/shard_map/while/body/eval_jaxpr/ppermute | solution.py:16
  350.9 17.9 %copy-start.5 = (f32[128,1]{0,1:T(1,128)S(1)}, f32[128,1]{0,1:T(1,128)}, u32[]{:S(2)}) copy-start(f32[128,1]{0,1:T(1,128)} %get-tuple-element.608) | copy-start | bytes 1540 | tf_op jit(solution)/shard_map/while
  371.2 6.1 %collective-permute-start = (bf16[16,4096]{1,0:T(8,128)(2,1)S(1)}, bf16[16,4096]{1,0:T(8,128)(2,1)S(1)}, u32[]{:S(2)}, u32[]{:S(2)}) collective-permute-start(bf16[16,4096]{1,0:T(8,128)(2,1)S(1)} %get-tuple-element.618), channel_id=1, source_target_pairs={{16,0},{17,1},{18,2},{19,3},{20,4},{21,5},{22,6},{23,7},{24,8},{25... | collective-permute-start | bytes 393224 | tf_op jit(solution)/shard_map/while/body/eval_jaxpr/ppermute | solution.py:16
  380.6 17.9 %copy-start.5 = (f32[128,1]{0,1:T(1,128)S(1)}, f32[128,1]{0,1:T(1,128)}, u32[]{:S(2)}) copy-start(f32[128,1]{0,1:T(1,128)} %get-tuple-element.608) | copy-start | bytes 1540 | tf_op jit(solution)/shard_map/while
  400.8 6.2 %collective-permute-start = (bf16[16,4096]{1,0:T(8,128)(2,1)S(1)}, bf16[16,4096]{1,0:T(8,128)(2,1)S(1)}, u32[]{:S(2)}, u32[]{:S(2)}) collective-permute-start(bf16[16,4096]{1,0:T(8,128)(2,1)S(1)} %get-tuple-element.618), channel_id=1, source_target_pairs={{16,0},{17,1},{18,2},{19,3},{20,4},{21,5},{22,6},{23,7},{24,8},{25... | collective-permute-start | bytes 393224 | tf_op jit(solution)/shard_map/while/body/eval_jaxpr/ppermute | solution.py:16
  410.3 10.5 %copy-start.5 = (f32[128,1]{0,1:T(1,128)S(1)}, f32[128,1]{0,1:T(1,128)}, u32[]{:S(2)}) copy-start(f32[128,1]{0,1:T(1,128)} %get-tuple-element.608) | copy-start | bytes 1540 | tf_op jit(solution)/shard_map/while
  420.9 15.8 %collective-permute-start = (bf16[16,4096]{1,0:T(8,128)(2,1)S(1)}, bf16[16,4096]{1,0:T(8,128)(2,1)S(1)}, u32[]{:S(2)}, u32[]{:S(2)}) collective-permute-start(bf16[16,4096]{1,0:T(8,128)(2,1)S(1)} %get-tuple-element.618), channel_id=1, source_target_pairs={{16,0},{17,1},{18,2},{19,3},{20,4},{21,5},{22,6},{23,7},{24,8},{25... | collective-permute-start | bytes 393224 | tf_op jit(solution)/shard_map/while/body/eval_jaxpr/ppermute | solution.py:16
  446.0 18.3 %copy-start.3 = (f32[2,1024]{1,0:T(2,128)}, f32[2,1024]{1,0:T(2,128)S(1)}, u32[]{:S(2)}) copy-start(f32[2,1024]{1,0:T(2,128)S(1)} %psum.22) | copy-start | bytes 24580
Sparse Core Ops, SparseCore 0:
  9.9 89.3 all-gather.1
  118.1 52.1 all-reduce.1
